TPU v7x, 32 devices: a whole 2x2x4 slice. The times are simulated.
32 devices in a mesh: wide: 8 (over y, x, core), narrow: 4 (over z).
Axes of the slice: x: 2, y: 2, z: 4, core: 2. Of those that a mesh axis runs over, the one named last changes fastest.
Arguments:
- pooled: bfloat16 [16384, 1024], P(('wide', 'narrow')), may hold values from -6 to 6
- cotangent: bfloat16 [16384, 512], P(('wide', 'narrow')), may hold values from -6 to 6
- w_first: bfloat16 [1024, 1024], P('narrow'), may hold values from -0.1875 to 0.1875
- b_first: float32 [1024], replicated, may hold values from -5 to 5
- w_second: bfloat16 [1024, 512], P('narrow'), may hold values from -0.1875 to 0.1875
- counts: bfloat16 [8, 64, 16384], P(None, 'narrow', 'wide'), may hold values from 0 to 3, as said below
- row_ids: int32 [8, 64], P(None, 'narrow'), may hold values from 0 to 63, as said below
- table: float32 [8, 256, 128], P(None, 'narrow'), may hold values from -6 to 6
- accum: float32 [8, 256, 128], P(None, 'narrow'), may hold values from 0.1 to 10
Outputs:
- new_table: float32 [8, 256, 128], P(None, 'narrow')
- new_accum: float32 [8, 256, 128], P(None, 'narrow')
Inputs may be any that keep to these rules, and one draw needn't show every extreme that they name: `counts`: each entry is zero where the sample does not look up the active row, else a positive lookup weight. `row_ids`: for each table, the 16 ids of one owner (slots j * 16 to (j + 1) * 16 - 1) are distinct.
All inputs are finite; a program needn't handle non-finite values.
Results may differ from a plain program's by a relative error of at most 0.0038.
Values may be sent and summed in bfloat16 or wider, within the bound.
A program may use at most 128 MiB of HBM per device.

v0:
```python
import math
import jax
import jax.numpy as jnp
from jax import lax
from jax.sharding import PartitionSpec as P

clip_factor = 0.5
learn_rate = 0.05
epsilon = 1e-08


def tower_back(inputs, cotangent, w_first, b_first, w_second):
    hidden_in = jnp.dot(inputs, w_first, preferred_element_type=jnp.float32) + b_first
    back_hidden = lax.dot_general(
        cotangent, w_second, (((1,), (1,)), ((), ())), preferred_element_type=jnp.float32
    )
    sigmoid_val = jax.nn.sigmoid(hidden_in)
    slopes = sigmoid_val * (1.0 + hidden_in * (1.0 - sigmoid_val))
    deltas = (back_hidden * slopes).astype(jnp.bfloat16)
    return lax.dot_general(
        deltas, w_first, (((1,), (1,)), ((), ())), preferred_element_type=jnp.float32
    ).astype(jnp.bfloat16)


def clip_rows(grads, limit):
    norms = jnp.sqrt(jnp.sum(grads * grads, axis=-1, keepdims=True))
    return grads * (limit / jnp.maximum(norms, limit))


def adagrad_rows(current, old_acc, summed):
    new_acc = old_acc + summed * summed
    return (current - learn_rate * summed / (jnp.sqrt(new_acc) + epsilon), new_acc)


def shards(pooled, cotangent, w_first, b_first, w_second, counts, row_ids, table, accum):
    full_first, full_second = (
        lax.all_gather(w_first, "narrow", axis=0, tiled=True),
        lax.all_gather(w_second, "narrow", axis=0, tiled=True),
    )
    grad_in = tower_back(pooled, cotangent, full_first, b_first, full_second)
    tables = counts.shape[0]
    slots = counts.shape[1]
    bags = counts.shape[2]
    emb = table.shape[2]
    samples = pooled.shape[0]
    scale = 1.0 / math.sqrt(bags)
    limit = clip_factor * math.sqrt(emb)
    regrouped = lax.all_to_all(counts, "narrow", split_axis=2, concat_axis=1, tiled=True)
    local_grad = grad_in.reshape(samples, tables, emb)
    grads = lax.psum_scatter(
        jnp.einsum(
            "tab,btd->atd", regrouped, local_grad, preferred_element_type=jnp.float32
        ).reshape(slots * lax.axis_size("narrow"), tables * emb),
        "narrow",
        scatter_dimension=0,
        tiled=True,
    ).reshape(slots, tables, emb)
    clipped = clip_rows(grads * scale, limit)
    table_index = jnp.arange(tables, dtype=jnp.int32)[:, None]
    current = jnp.transpose(table[table_index, row_ids], (1, 0, 2))
    old_acc = jnp.transpose(accum[table_index, row_ids], (1, 0, 2))
    summed = lax.psum(clipped, "wide")
    new_rows, new_acc = adagrad_rows(current, old_acc, summed)
    new_table = table.at[table_index, row_ids].set(jnp.transpose(new_rows, (1, 0, 2)))
    new_accum = accum.at[table_index, row_ids].set(jnp.transpose(new_acc, (1, 0, 2)))
    return (new_table, new_accum)


def solution(mesh):
    in_specs = (
        P(("wide", "narrow"), None),
        P(("wide", "narrow"), None),
        P("narrow", None),
        P(),
        P("narrow", None),
        P(None, "narrow", "wide"),
        P(None, "narrow"),
        P(None, "narrow", None),
        P(None, "narrow", None),
    )
    out_specs = (P(None, "narrow", None), P(None, "narrow", None))
    return jax.shard_map(shards, mesh=mesh, in_specs=in_specs, out_specs=out_specs, check_vma=False)
```

profile of v0, /device:TPU:0, one launch (start us, length us, event | category | flops | bytes accessed | tf_op | source)
XLA Modules:
  0.0 199.6 jit_solution(9209073839710677612)
XLA Ops:
  7.2 0.0 copy-start
  7.2 0.0 copy-start.3
  7.2 0.0 all-gather.5.cloned.1.call-start
  7.2 1.1 copy.53
  8.3 0.9 copy.54
  9.3 0.0 all-gather.5.cloned.1.call-update
  9.3 0.0 all-gather.3.cloned.1.call-start
  9.3 0.7 all-gather.3.cloned.1.call-update
  10.0 0.0 reduce-scatter.2.cloned.1.call-start
  10.1 0.0 copy-done.3
  10.1 4.2 %copy.26 = bf16[8,16,2048]{1,0,2:T(8,128)(2,1)} copy(bf16[8,16,2048]{2,1,0:T(8,128)(2,1)S(1)} %copy-done.3) | data formatting | bytes 1048576 | tf_op args[5]
  14.3 5.8 %reshape.51 = bf16[4,2,32768]{2,1,0:T(2,128)(2,1)S(1)} reshape(bf16[2048,8,16]{2,1,0:T(8,128)(2,1)} %bitcast.58) | data formatting | bytes 1048576
  20.1 35.4 %all_to_all.18 = bf16[4,2,32768]{2,1,0:T(2,128)(2,1)S(1)} all-to-all(bf16[4,2,32768]{2,1,0:T(2,128)(2,1)S(1)} %reshape.51), channel_id=1, replica_groups=mesh['wide'=8,'narrow'=4] {'narrow'}, dimensions={0} | all-to-all | bytes 1048576 | tf_op jit(solution)/shard_map/all_to_all | solution.py:48
  55.5 4.1 %reshape.52 = bf16[2048,8,16]{2,1,0:T(8,128)(2,1)} reshape(bf16[4,2,32768]{2,1,0:T(2,128)(2,1)S(1)} %all_to_all.18) | data formatting | bytes 1048576
  59.7 4.4 %copy.27 = bf16[8,16,4,512]{3,1,2,0:T(8,128)(2,1)S(1)} copy(bf16[8,16,4,512]{1,0,3,2:T(8,128)(2,1)} %bitcast.57) | data formatting | bytes 1048576 | tf_op jit(solution)/shard_map/all_to_all | solution.py:48
  64.1 0.0 copy-start.5
  64.1 5.2 %all-gather.5.cloned.1.call-done = bf16[1024,1024]{1,0:T(8,128)(2,1)} async-done(((bf16[256,1024]{1,0:T(8,128)(2,1)}), bf16[1024,1024]{1,0:T(8,128)(2,1)}) %all-gather.5.cloned.1.call-update) | async-done | bytes 2097168 | tf_op jit(solution)/shard_map/all_gather | solution.py:37
  69.2 0.0 copy-done
  69.2 4.2 %fusion.13 = f32[512,1024]{1,0:T(8,128)} fusion(bf16[512,1024]{1,0:T(8,128)(2,1)S(1)} %copy-done, bf16[1024,1024]{1,0:T(8,128)(2,1)} %all-gather.5.cloned.1.call-done), kind=kOutput, calls=%fused_computation.32 | convolution fusion | flops 1073741824 | bytes 5242880 | tf_op jit(solution)/shard_map/dot_general | solution.py:13
  73.4 24.1 %all-gather.3.cloned.1.call-done = bf16[1024,512]{1,0:T(8,128)(2,1)} async-done(((bf16[256,512]{1,0:T(8,128)(2,1)}), bf16[1024,512]{1,0:T(8,128)(2,1)}) %all-gather.3.cloned.1.call-update) | async-done | bytes 1048592 | tf_op jit(solution)/shard_map/all_gather | solution.py:38
  97.5 0.0 copy-done.5
  97.5 4.6 %fusion = bf16[64,8,8,128]{3,2,1,0:T(8,128)(2,1)S(1)} fusion(bf16[1024,1024]{1,0:T(8,128)(2,1)} %all-gather.5.cloned.1.call-done, f32[512,1024]{1,0:T(8,128)} %fusion.13, bf16[512,512]{1,0:T(8,128)(2,1)} %param.10, bf16[1024,512]{1,0:T(8,128)(2,1)} %all-gather.3.cloned.1.call-done, f32[1024]{0:T(1024)S(1)} %copy-done.5), kind=kOutput, calls=%fused_computation.6 | convolution fusion | flops 1616379904 | bytes 6819840 | tf_op jit(solution)/shard_map/dot_general | solution.py:20
  102.0 0.0 copy-start.4
  102.1 0.3 convolution_bitcast_fusion
  102.4 0.7 copy.47
  103.1 0.0 reduce-scatter.2.cloned.1.call-update
  103.1 0.0 all-reduce.2.cloned.1.call-start
  103.2 19.5 %reduce-scatter.2.cloned.1.call-done = f32[16,1024]{1,0:T(8,128)} async-done(((f32[64,1024]{1,0:T(8,128)}), f32[16,1024]{1,0:T(8,128)}) %reduce-scatter.2.cloned.1.call-update) | async-done | bytes 65552 | tf_op jit(solution)/shard_map/reduce_scatter | solution.py:50
  122.7 0.9 copy.35
  123.6 0.1 multiply_reduce_fusion
  123.7 0.7 bitcast_multiply_fusion
  124.4 0.0 all-reduce.2.cloned.1.call-update
  124.4 0.0 copy-done.4
  124.4 0.1 reshape.27
  124.5 1.2 gather_fusion
  125.7 1.2 gather_fusion.1
  127.0 0.1 reshape.39
  127.1 50.5 %all-reduce.2.cloned.1.call-done = f32[16,8,128]{2,1,0:T(8,128)} async-done(((f32[16,8,128]{2,1,0:T(8,128)}), f32[16,8,128]{2,1,0:T(8,128)}) %all-reduce.2.cloned.1.call-update) | async-done | bytes 65552 | tf_op jit(solution)/shard_map/psum | solution.py:62
  177.6 0.9 fusion.6
  178.6 6.9 %scatter_fusion.1 = f32[8,64,128]{2,1,0:T(8,128)S(1)} fusion(f32[8,64,128]{2,1,0:T(8,128)S(1)} %copy.54, s32[128]{0:T(128)S(1)} %reshape.39, f32[128,128]{1,0:T(8,128)S(1)} %bitcast.64), kind=kCustom, calls=%fused_computation.3 | custom fusion | bytes 197632 | tf_op jit(solution)/shard_map/scatter | solution.py:65
  185.5 0.0 copy-start.2
  185.5 6.9 %scatter_fusion = f32[8,64,128]{2,1,0:T(8,128)S(1)} fusion(f32[8,64,128]{2,1,0:T(8,128)S(1)} %copy.53, s32[128]{0:T(128)S(1)} %reshape.39, f32[128,128]{1,0:T(8,128)S(1)} %bitcast.63), kind=kCustom, calls=%fused_computation.2 | custom fusion | bytes 197632 | tf_op jit(solution)/shard_map/scatter | solution.py:64
  192.4 0.0 copy-done.2
  192.4 0.0 copy-start.1
  192.4 0.7 copy-done.1
  (5 shorter events, 0.1 us)
Async XLA Ops:
  7.2 62.1 %copy-start = (bf16[512,1024]{1,0:T(8,128)(2,1)S(1)}, bf16[512,1024]{1,0:T(8,128)(2,1)}, u32[]{:S(2)}) copy-start(bf16[512,1024]{1,0:T(8,128)(2,1)} %param.9) | copy-start | bytes 3145732
  7.2 2.9 %copy-start.3 = (bf16[8,16,2048]{2,1,0:T(8,128)(2,1)S(1)}, bf16[8,16,2048]{2,1,0:T(8,128)(2,1)}, u32[]{:S(2)}) copy-start(bf16[8,16,2048]{2,1,0:T(8,128)(2,1)} %param.14) | copy-start | bytes 1572868
  7.2 62.0 %all-gather.5.cloned.1.call-start = ((), (), s32[]{:S(2)}) async-start(), calls=%async_computation.3 | async-start | bytes 2621440 | tf_op jit(solution)/shard_map/all_gather | solution.py:37
  9.3 88.2 %all-gather.3.cloned.1.call-start = ((), (), s32[]{:S(2)}) async-start(), calls=%async_computation.2 | async-start | bytes 1310720 | tf_op jit(solution)/shard_map/all_gather | solution.py:38
  10.0 112.6 %reduce-scatter.2.cloned.1.call-start = ((), (), s32[]{:S(2)}) async-start(), calls=%async_computation.4 | async-start | bytes 327680 | tf_op jit(solution)/shard_map/reduce_scatter | solution.py:50
  64.1 33.4 %copy-start.5 = (f32[1024]{0:T(1024)S(1)}, f32[1024]{0:T(1024)}, u32[]{:S(2)}) copy-start(f32[1024]{0:T(1024)} %param.12) | copy-start | bytes 12292
  102.0 22.4 %copy-start.4 = (s32[8,16]{1,0:T(8,128)S(1)}, s32[8,16]{1,0:T(8,128)}, u32[]{:S(2)}) copy-start(s32[8,16]{1,0:T(8,128)} %param.15) | copy-start | bytes 1540
  103.1 74.5 %all-reduce.2.cloned.1.call-start = ((), (), s32[]{:S(2)}) async-start(), calls=%async_computation.5 | async-start | bytes 131072 | tf_op jit(solution)/shard_map/psum | solution.py:62
  185.5 6.9 %copy-start.2 = (f32[8,64,128]{2,1,0:T(8,128)}, f32[8,64,128]{2,1,0:T(8,128)S(1)}, u32[]{:S(2)}) copy-start(f32[8,64,128]{2,1,0:T(8,128)S(1)} %scatter_fusion.1) | copy-start | bytes 786436
  192.4 0.7 copy-start.1
Sparse Core Ops, SparseCore 0:
  9.6 59.6 all-gather.4
  70.8 26.6 all-gather.2
  103.3 19.3 reduce-scatter.1
  126.2 51.3 all-reduce.1
where the time goes:
time: 200 us
  waiting for transfers between devices  100 us (50%)
  local copies, waits for them, and re-layouts  39.3 us (20%)
  blocking collectives  35.4 us (18%)
  between operations  13.9 us (7%)
  matrix products  9.06 us (5%)
    psum x1, waiting for transfers between devices, shards(): summed = lax.psum(clipped, 'wide')  50.5 us
    all_to_all x1, blocking collectives, shards(): lax.all_to_all(counts, 'narrow', split_axis=2, concat_axis=1, tiled=True)  35.4 us
    all_gather x1, waiting for transfers between devices, shards(): lax.all_gather(w_second, 'narrow', axis=0, tiled=True)  24.1 us
    reduce_scatter x1, waiting for transfers between devices, shards(): lax.psum_scatter(jnp.einsum('tab,btd->atd', regrouped, local_grad, prefer...  19.5 us
    unnamed x18, local copies, waits for them, and re-layouts  17.7 us
    scatter x1, local copies, waits for them, and re-layouts, shards(): accum.at[table_index, row_ids].set(jnp.transpose(new_acc, (1, 0, 2)))  6.9 us
    scatter x1, local copies, waits for them, and re-layouts, shards(): table.at[table_index, row_ids].set(jnp.transpose(new_rows, (1, 0, 2)))  6.9 us
    all_gather x1, waiting for transfers between devices, shards(): lax.all_gather(w_first, 'narrow', axis=0, tiled=True)  5.15 us
  transfers between devices with their start and end apart: 4, of which 4 were waited for; matrix products, arithmetic and copies ran while one was open for 13% of the time, Pallas kernels for 0%

commit v1 on v0

--- a/solution.py
+++ b/solution.py
@@ -59,7 +59,12 @@
     table_index = jnp.arange(tables, dtype=jnp.int32)[:, None]
     current = jnp.transpose(table[table_index, row_ids], (1, 0, 2))
     old_acc = jnp.transpose(accum[table_index, row_ids], (1, 0, 2))
-    summed = lax.psum(clipped, "wide")
+
+    def run_direct(slab_in):
+        r1 = jax.lax.all_gather(slab_in, "wide").sum(axis=0)
+        return r1
+
+    summed = run_direct(clipped)
     new_rows, new_acc = adagrad_rows(current, old_acc, summed)
     new_table = table.at[table_index, row_ids].set(jnp.transpose(new_rows, (1, 0, 2)))
     new_accum = accum.at[table_index, row_ids].set(jnp.transpose(new_acc, (1, 0, 2)))

time: 200 us -> 156 us (0.78)
  waiting for transfers between devices: 100 us -> 46.9 us
  blocking collectives: 35.4 us -> 45.3 us
    psum x1 -> x0, waiting for transfers between devices: 50.5 us -> none  [shards(): summed = lax.psum(clipped, 'wide')]
    all_gather x0 -> x1, blocking collectives: none -> 9.8 us  [run_direct(): r1 = jax.lax.all_gather(slab_in, 'wide').sum(axis=0)]
    reduce_scatter x1, waiting for transfers between devices: 19.5 us -> 16.9 us  [shards(): lax.psum_scatter(jnp.einsum('tab,btd->atd', regrouped, local_grad, prefer...]
    unnamed x18 -> x19, local copies, waits for them, and re-layouts: 17.7 us -> 17.7 us
  transfers between devices with their start and end apart: 4 -> 3, of which waited for: 4 -> 3; matrix products, arithmetic and copies ran while one was open for 13% -> 16% of each run, Pallas kernels for 0% -> 0%
where the time goes in v1:
time: 156 us
  waiting for transfers between devices  46.9 us (30%)
  blocking collectives  45.3 us (29%)
  local copies, waits for them, and re-layouts  39.3 us (25%)
  between operations  13.9 us (9%)
  matrix products  9.04 us (6%)
    all_to_all x1, blocking collectives, shards(): lax.all_to_all(counts, 'narrow', split_axis=2, concat_axis=1, tiled=True)  35.4 us
    all_gather x1, waiting for transfers between devices, shards(): lax.all_gather(w_second, 'narrow', axis=0, tiled=True)  24.1 us
    unnamed x19, local copies, waits for them, and re-layouts  17.7 us
    reduce_scatter x1, waiting for transfers between devices, shards(): lax.psum_scatter(jnp.einsum('tab,btd->atd', regrouped, local_grad, prefer...  16.9 us
    all_gather x1, blocking collectives, run_direct(): r1 = jax.lax.all_gather(slab_in, 'wide').sum(axis=0)  9.8 us
    scatter x1, local copies, waits for them, and re-layouts, shards(): accum.at[table_index, row_ids].set(jnp.transpose(new_acc, (1, 0, 2)))  6.9 us
    scatter x1, local copies, waits for them, and re-layouts, shards(): table.at[table_index, row_ids].set(jnp.transpose(new_rows, (1, 0, 2)))  6.9 us
    all_gather x1, waiting for transfers between devices, shards(): lax.all_gather(w_first, 'narrow', axis=0, tiled=True)  5.18 us
  transfers between devices with their start and end apart: 3, of which 3 were waited for; matrix products, arithmetic and copies ran while one was open for 16% of the time, Pallas kernels for 0%

profile of v1, /device:TPU:0, one launch (start us, length us, event | category | flops | bytes accessed | tf_op | source)
XLA Modules:
  0.0 155.6 jit_solution(11841349045288366326)
XLA Ops:
  7.2 0.0 copy-start
  7.2 0.0 copy-start.3
  7.2 0.0 all-gather.5.cloned.1.call-start
  7.2 1.1 copy.47
  8.3 0.9 copy.48
  9.3 0.0 all-gather.5.cloned.1.call-update
  9.3 0.0 all-gather.3.cloned.1.call-start
  9.3 0.7 all-gather.3.cloned.1.call-update
  10.0 0.0 reduce-scatter.2.cloned.1.call-start
  10.1 0.0 copy-done.3
  10.1 4.2 %copy.22 = bf16[8,16,2048]{1,0,2:T(8,128)(2,1)} copy(bf16[8,16,2048]{2,1,0:T(8,128)(2,1)S(1)} %copy-done.3) | data formatting | bytes 1048576 | tf_op args[5]
  14.3 5.8 %reshape.64 = bf16[4,2,32768]{2,1,0:T(2,128)(2,1)S(1)} reshape(bf16[2048,8,16]{2,1,0:T(8,128)(2,1)} %bitcast.55) | data formatting | bytes 1048576
  20.1 35.4 %all_to_all.18 = bf16[4,2,32768]{2,1,0:T(2,128)(2,1)S(1)} all-to-all(bf16[4,2,32768]{2,1,0:T(2,128)(2,1)S(1)} %reshape.64), channel_id=1, replica_groups=mesh['wide'=8,'narrow'=4] {'narrow'}, dimensions={0} | all-to-all | bytes 1048576 | tf_op jit(solution)/shard_map/all_to_all | solution.py:48
  55.5 4.1 %reshape.65 = bf16[2048,8,16]{2,1,0:T(8,128)(2,1)} reshape(bf16[4,2,32768]{2,1,0:T(2,128)(2,1)S(1)} %all_to_all.18) | data formatting | bytes 1048576
  59.6 4.4 %copy.23 = bf16[8,16,4,512]{3,1,2,0:T(8,128)(2,1)S(1)} copy(bf16[8,16,4,512]{1,0,3,2:T(8,128)(2,1)} %bitcast.54) | data formatting | bytes 1048576 | tf_op jit(solution)/shard_map/all_to_all | solution.py:48
  64.0 0.0 copy-start.5
  64.0 5.2 %all-gather.5.cloned.1.call-done = bf16[1024,1024]{1,0:T(8,128)(2,1)} async-done(((bf16[256,1024]{1,0:T(8,128)(2,1)}), bf16[1024,1024]{1,0:T(8,128)(2,1)}) %all-gather.5.cloned.1.call-update) | async-done | bytes 2097168 | tf_op jit(solution)/shard_map/all_gather | solution.py:37
  69.2 0.0 copy-done
  69.2 4.2 %fusion.12 = f32[512,1024]{1,0:T(8,128)} fusion(bf16[512,1024]{1,0:T(8,128)(2,1)S(1)} %copy-done, bf16[1024,1024]{1,0:T(8,128)(2,1)} %all-gather.5.cloned.1.call-done), kind=kOutput, calls=%fused_computation.30 | convolution fusion | flops 1073741824 | bytes 5242880 | tf_op jit(solution)/shard_map/dot_general | solution.py:13
  73.4 24.1 %all-gather.3.cloned.1.call-done = bf16[1024,512]{1,0:T(8,128)(2,1)} async-done(((bf16[256,512]{1,0:T(8,128)(2,1)}), bf16[1024,512]{1,0:T(8,128)(2,1)}) %all-gather.3.cloned.1.call-update) | async-done | bytes 1048592 | tf_op jit(solution)/shard_map/all_gather | solution.py:38
  97.5 0.0 copy-done.5
  97.5 4.6 %fusion = bf16[64,8,8,128]{3,2,1,0:T(8,128)(2,1)S(1)} fusion(bf16[1024,1024]{1,0:T(8,128)(2,1)} %all-gather.5.cloned.1.call-done, f32[512,1024]{1,0:T(8,128)} %fusion.12, bf16[512,512]{1,0:T(8,128)(2,1)} %param.10, bf16[1024,512]{1,0:T(8,128)(2,1)} %all-gather.3.cloned.1.call-done, f32[1024]{0:T(1024)S(1)} %copy-done.5), kind=kOutput, calls=%fused_computation.6 | convolution fusion | flops 1616379904 | bytes 6819840 | tf_op jit(solution)/shard_map/dot_general | solution.py:20
  102.0 0.0 copy-start.4
  102.1 0.3 convolution_bitcast_fusion
  102.4 0.7 copy.42
  103.1 0.0 reduce-scatter.2.cloned.1.call-update
  103.1 0.0 copy-done.4
  103.2 0.1 reshape.40
  103.2 1.2 gather_fusion
  104.5 1.2 gather_fusion.1
  105.7 0.1 reshape.52
  105.8 16.9 %reduce-scatter.2.cloned.1.call-done = f32[16,1024]{1,0:T(8,128)} async-done(((f32[64,1024]{1,0:T(8,128)}), f32[16,1024]{1,0:T(8,128)}) %reduce-scatter.2.cloned.1.call-update) | async-done | bytes 65552 | tf_op jit(solution)/shard_map/reduce_scatter | solution.py:50
  122.7 0.8 multiply_bitcast_fusion
  123.5 0.1 reduce_sum.18
  123.7 0.9 copy.32
  124.5 0.1 bitcast_multiply_fusion
  124.6 9.8 %all_gather.12 = f32[8,16,8,128]{3,2,1,0:T(8,128)S(1)} all-gather(f32[1,16,8,128]{3,2,1,0:T(8,128)S(1)} %bitcast_multiply_fusion), channel_id=1, replica_groups=mesh['wide'=8,'narrow'=4] {'wide'}, dimensions={0}, use_global_device_ids=true | all-gather | bytes 589824 | tf_op jit(solution)/shard_map/all_gather | solution.py:64
  134.4 0.1 fusion.5
  134.6 6.9 %scatter_fusion.1 = f32[8,64,128]{2,1,0:T(8,128)S(1)} fusion(f32[8,64,128]{2,1,0:T(8,128)S(1)} %copy.48, s32[128]{0:T(128)S(1)} %reshape.52, f32[128,128]{1,0:T(8,128)S(1)} %bitcast.61), kind=kCustom, calls=%fused_computation.3 | custom fusion | bytes 197632 | tf_op jit(solution)/shard_map/scatter | solution.py:70
  141.5 0.0 copy-start.2
  141.5 6.9 %scatter_fusion = f32[8,64,128]{2,1,0:T(8,128)S(1)} fusion(f32[8,64,128]{2,1,0:T(8,128)S(1)} %copy.47, s32[128]{0:T(128)S(1)} %reshape.52, f32[128,128]{1,0:T(8,128)S(1)} %bitcast.60), kind=kCustom, calls=%fused_computation.2 | custom fusion | bytes 197632 | tf_op jit(solution)/shard_map/scatter | solution.py:69
  148.4 0.0 copy-done.2
  148.4 0.0 copy-start.1
  148.4 0.7 copy-done.1
  (6 shorter events, 0.1 us)
Async XLA Ops:
  7.2 62.1 %copy-start = (bf16[512,1024]{1,0:T(8,128)(2,1)S(1)}, bf16[512,1024]{1,0:T(8,128)(2,1)}, u32[]{:S(2)}) copy-start(bf16[512,1024]{1,0:T(8,128)(2,1)} %param.9) | copy-start | bytes 3145732
  7.2 2.9 %copy-start.3 = (bf16[8,16,2048]{2,1,0:T(8,128)(2,1)S(1)}, bf16[8,16,2048]{2,1,0:T(8,128)(2,1)}, u32[]{:S(2)}) copy-start(bf16[8,16,2048]{2,1,0:T(8,128)(2,1)} %param.14) | copy-start | bytes 1572868
  7.2 62.0 %all-gather.5.cloned.1.call-start = ((), (), s32[]{:S(2)}) async-start(), calls=%async_computation.3 | async-start | bytes 2621440 | tf_op jit(solution)/shard_map/all_gather | solution.py:37
  9.3 88.2 %all-gather.3.cloned.1.call-start = ((), (), s32[]{:S(2)}) async-start(), calls=%async_computation.2 | async-start | bytes 1310720 | tf_op jit(solution)/shard_map/all_gather | solution.py:38
  10.0 112.6 %reduce-scatter.2.cloned.1.call-start = ((), (), s32[]{:S(2)}) async-start(), calls=%async_computation.4 | async-start | bytes 327680 | tf_op jit(solution)/shard_map/reduce_scatter | solution.py:50
  64.0 33.5 %copy-start.5 = (f32[1024]{0:T(1024)S(1)}, f32[1024]{0:T(1024)}, u32[]{:S(2)}) copy-start(f32[1024]{0:T(1024)} %param.12) | copy-start | bytes 12292
  102.0 1.1 copy-start.4
  141.5 6.9 %copy-start.2 = (f32[8,64,128]{2,1,0:T(8,128)}, f32[8,64,128]{2,1,0:T(8,128)S(1)}, u32[]{:S(2)}) copy-start(f32[8,64,128]{2,1,0:T(8,128)S(1)} %scatter_fusion.1) | copy-start | bytes 786436
  148.4 0.7 copy-start.1
Sparse Core Ops, SparseCore 0:
  9.6 59.6 all-gather.4
  70.8 26.6 all-gather.2
  103.3 19.3 reduce-scatter.1
